TPU v7x, 256 devices: a whole 4x4x8 slice. The times are simulated.
256 devices in a mesh: dp: 64 (over x, z, core), grp: 4 (over y).
Axes of the slice: x: 4, y: 4, z: 8, core: 2. Of those that a mesh axis runs over, the one named last changes fastest.
Arguments:
- embeddings: bfloat16 [8192, 64, 1024], P('dp', None, 'grp'), may hold values from -17 to 17
- lengths: int32 [8192], P('dp'), may hold values from 1 to 64
- parent_slot: int32 [8192], P('dp'), may hold values from 0 to 8191, as said below
- centroids: bfloat16 [8192, 16, 1024], P('dp', None, 'grp'), may hold values from -17 to 17
Outputs:
- refined: bfloat16 [8192, 16, 1024], P('dp', None, 'grp')
Inputs may be any that keep to these rules, and one draw needn't show every extreme that they name: `parent_slot`: each parent has its own slot; slot // 128 is the index of dp that keeps that parent's centroids; the parents of one index of dp are kept by exactly 32 indices of dp, 4 by each. Rows past lengths[p] in a block are padding.
All inputs are finite; a program needn't handle non-finite values.
Results may differ from a plain program's by a relative error of at most 0.0057.
Values may be sent and summed in bfloat16 or wider, within the bound.
A program may use at most 128 MiB of HBM per device.

v0:
```python
import jax
import jax.numpy as jnp
from jax import lax
from jax.sharding import PartitionSpec as P

ITERS = 2


assignment_sharpness = 0.02
prior_weight = 1.0
epsilon = 1e-06


def row_totals(values):
    return lax.psum(values, "grp")


def part_totals(cosine_similarity_matrix, centre_sq):
    return lax.psum((cosine_similarity_matrix, centre_sq), "grp")


def refine(vectors, live_rows, start):
    own_sq = jnp.einsum("pbd,pbd->pb", vectors, vectors, preferred_element_type=jnp.float32)
    sample_norm_multiplier = lax.rsqrt(row_totals(own_sq) + epsilon)
    current = start
    for step in range(ITERS):
        cosine_similarity_matrix = jnp.einsum(
            "pkd,pbd->pkb", current, vectors, preferred_element_type=jnp.float32
        )
        centre_sq = jnp.einsum("pkd,pkd->pk", current, current, preferred_element_type=jnp.float32)
        cosine_similarity_matrix, centre_sq = part_totals(cosine_similarity_matrix, centre_sq)
        cluster_mean_norm_multiplier = lax.rsqrt(centre_sq + epsilon)
        membership_logits = (
            cosine_similarity_matrix
            * cluster_mean_norm_multiplier[:, :, None]
            * sample_norm_multiplier[:, None, :]
            / assignment_sharpness
        )
        raised = jnp.exp(membership_logits)
        weights = jnp.where(
            live_rows[:, None, :], raised / jnp.sum(raised, axis=1, keepdims=True), 0.0
        ).astype(jnp.bfloat16)
        moments = jnp.einsum("pkb,pbd->pkd", weights, vectors, preferred_element_type=jnp.float32)
        totals = jnp.sum(weights.astype(jnp.float32), axis=2)
        current = (
            (moments + prior_weight * current.astype(jnp.float32))
            / (totals + prior_weight)[:, :, None]
        ).astype(jnp.bfloat16)
    return current


def on_device(embeddings, lengths, parent_slot, centroids):
    parents, block_rows, width_part = embeddings.shape
    peers = lax.axis_size("dp")
    capacity = 2 * parents // peers
    holder = parent_slot // parents
    local_slot = parent_slot - holder * parents
    matches = (holder[:, None] == jnp.arange(peers, dtype=jnp.int32)[None, :]).astype(jnp.int32)
    incoming_order = jnp.sum((jnp.cumsum(matches, axis=0) - matches) * matches, axis=1)
    slots = (
        jnp.full((peers, capacity), parents, jnp.int32).at[holder, incoming_order].set(local_slot)
    )
    sizes = jnp.zeros((peers, capacity), jnp.int32).at[holder, incoming_order].set(lengths)
    blocks = (
        jnp.zeros((peers, capacity, block_rows, width_part), jnp.bfloat16)
        .at[holder, incoming_order]
        .set(embeddings)
    )
    got_blocks, got_sizes, received_slot_list = (
        lax.all_to_all(blocks, "dp", split_axis=0, concat_axis=0, tiled=True),
        lax.all_to_all(sizes, "dp", split_axis=0, concat_axis=0, tiled=True),
        lax.all_to_all(slots, "dp", split_axis=0, concat_axis=0, tiled=True),
    )
    flat_slots = received_slot_list.reshape(-1)
    vectors = got_blocks.reshape(peers * capacity, block_rows, width_part)
    live_rows = jnp.arange(block_rows)[None, :] < got_sizes.reshape(-1)[:, None]
    start = jnp.take(centroids, flat_slots, axis=0, mode="fill", fill_value=0)
    updated_output = refine(vectors, live_rows, start)
    return jnp.zeros_like(centroids).at[flat_slots].set(updated_output, mode="drop")


def solution(mesh):
    return jax.shard_map(
        on_device,
        mesh=mesh,
        in_specs=(P("dp", None, "grp"), P("dp"), P("dp"), P("dp", None, "grp")),
        out_specs=P("dp", None, "grp"),
        check_vma=False,
    )
```

profile of v0, /device:TPU:1, one launch (start us, length us, event | category | flops | bytes accessed | tf_op | source)
XLA Modules:
  0.0 453.5 jit_solution(11371672327628218161)
XLA Ops:
  6.5 0.8 multiply_subtract_fusion
  7.8 6.5 %scatter_fusion = s32[64,4]{0,1:T(4,128)S(1)} fusion(s32[64,4]{0,1:T(4,128)S(1)} %broadcast_in_dim.37, s32[128]{0:T(128)S(1)} %fusion.12, s32[128]{0:T(128)S(1)} %get-tuple-element.11), kind=kCustom, calls=%fused_computation.1 | custom fusion | bytes 2560 | tf_op jit(solution)/shard_map/scatter | solution.py:61
  14.2 0.7 copy.8
  14.9 13.0 %all-to-all-start = ((s32[64,1,4]{2,1,0:T(1,128)}), s32[64,1,4]{2,1,0:T(1,128)S(1)}, u32[]{:S(2)}, u32[]{:S(2)}) async-start(s32[64,1,4]{2,1,0:T(1,128)} %copy.8), calls=%async_computation | async-start | bytes 65536 | tf_op jit(solution)/shard_map/all_to_all | solution.py:72
  27.9 4.3 broadcast_in_dim.67
  32.2 20.8 %scatter_fusion.2 = bf16[64,4,64,256]{3,2,1,0:T(8,128)(2,1)} fusion(bf16[64,4,64,256]{3,2,1,0:T(8,128)(2,1)} %broadcast_in_dim.67, s32[128]{0:T(128)S(1)} %fusion.12, bf16[128,64,256]{2,1,0:T(8,128)(2,1)} %param.4), kind=kCustom, calls=%fused_computation.3 | custom fusion | bytes 12583936 | tf_op jit(solution)/shard_map/scatter | solution.py:67
  52.9 10.5 %all-to-all-start.2 = ((bf16[64,4,64,256]{3,2,1,0:T(8,128)(2,1)}), bf16[64,4,64,256]{3,2,1,0:T(8,128)(2,1)}, u32[]{:S(2)}, u32[]{:S(2)}) async-start(bf16[64,4,64,256]{3,2,1,0:T(8,128)(2,1)} %scatter_fusion.2), calls=%async_computation.2 | async-start | bytes 16777216 | tf_op jit(solution)/shard_map/all_to_all | solution.py:70
  64.0 0.6 reduce.14
  64.9 0.8 gather_fusion
  65.7 183.5 %all-to-all-done.2 = bf16[64,4,64,256]{3,2,1,0:T(8,128)(2,1)} async-done(((bf16[64,4,64,256]{3,2,1,0:T(8,128)(2,1)}), bf16[64,4,64,256]{3,2,1,0:T(8,128)(2,1)}, u32[]{:S(2)}, u32[]{:S(2)}) %all-to-all-start.2) | async-done | bytes 8388640 | tf_op jit(solution)/shard_map/all_to_all | solution.py:70
  249.2 6.3 %fusion = f32[256,64]{1,0:T(8,128)} fusion(bf16[256,64,256]{2,1,0:T(8,128)(2,1)} %bitcast.6), kind=kLoop, calls=%fused_computation.6 | loop fusion | flops 12566528 | bytes 8454144 | tf_op jit(solution)/shard_map/pbd,pbd->pb/dot_general | solution.py:23
  255.5 7.0 %fusion.13 = f32[256,16,64]{2,1,0:T(8,128)} fusion(bf16[256,64,256]{2,1,0:T(8,128)(2,1)} %bitcast.6, bf16[256,16,256]{2,1,0:T(8,128)(2,1)S(1)} %gather_fusion, pred[256]{0:T(512)(128)(4,1)S(1)} %compare_and_fusion), kind=kOutput, calls=%fused_computation.52 | convolution fusion | flops 135266304 | bytes 11534592 | tf_op jit(solution)/shard_map/pkd,pbd->pkb/dot_general | solution.py:27
  263.2 6.5 %scatter_fusion.1 = s32[64,4]{0,1:T(4,128)S(1)} fusion(s32[64,4]{0,1:T(4,128)S(1)} %broadcast_in_dim.63, s32[128]{0:T(128)S(1)} %fusion.12, s32[128]{0:T(128)S(1)} %copy-done.6), kind=kCustom, calls=%fused_computation.2 | custom fusion | bytes 2560 | tf_op jit(solution)/shard_map/scatter | solution.py:63
  269.7 14.9 %all_to_all.23 = s32[64,1,4]{2,1,0:T(1,128)S(1)} all-to-all(s32[64,1,4]{2,1,0:T(1,128)S(1)} %copy.9), channel_id=1, replica_groups=mesh['dp'=64,'grp'=4] {'dp'}, dimensions={0} | all-to-all | bytes 2048 | tf_op jit(solution)/shard_map/all_to_all | solution.py:71
  284.6 0.6 reduce.15
  285.4 1.7 fusion.1
  287.1 15.0 %psum.36 = f32[256,16]{1,0:T(8,128)S(1)} all-reduce(f32[256,16]{1,0:T(8,128)S(1)} %fusion.1), channel_id=1, replica_groups=mesh['dp'=64,'grp'=4] {'grp'}, use_global_device_ids=true, to_apply=%region_6.7 | all-reduce | flops 4096 | bytes 32768 | tf_op jit(solution)/shard_map/psum | solution.py:19
  302.1 0.7 iota_compare_fusion
  302.8 23.1 %all-reduce.6.cloned.1.call-done = (f32[256,16,64]{2,1,0:T(8,128)}, f32[256,64]{1,0:T(8,128)}) async-done(((f32[256,16,64]{2,1,0:T(8,128)}, f32[256,64]{1,0:T(8,128)}), (f32[256,16,64]{2,1,0:T(8,128)}, f32[256,64]{1,0:T(8,128)})) %all-reduce.6.cloned.1.call-update) | async-done | bytes 1114128 | tf_op jit(solution)/shard_map/psum | solution.py:19
  326.0 1.1 add_rsqrt_fusion.1
  327.1 2.8 fusion.7
  329.9 1.7 convert_reduce_fusion.1
  331.7 4.6 %fusion.4 = (f32[256,16]{1,0:T(8,128)S(1)}, bf16[256,16,256]{2,1,0:T(8,128)(2,1)S(1)}) fusion(f32[256,16]{1,0:T(8,128)S(1)} %broadcast_add_fusion.1, bf16[256,16,256]{2,1,0:T(8,128)(2,1)S(1)} %gather_fusion, pred[256]{0:T(512)(128)(4,1)S(1)} %compare_and_fusion, bf16[256,16,64]{2,1,0:T(8,128)(2,1)S(1)} %get-tuple-element.10, bf16[256,64,256]{2,1,0:T(8,128)(2,1)} %bitcast.6), kind=kOutput, calls=%fused_computation.14 | convolution fusion | flops 142602240 | bytes 13140224 | tf_op jit(solution)/shard_map/pkb,pbd->pkd/dot_general | solution.py:43
  336.3 1.4 copy-done.3
  337.6 7.1 %fusion.14 = f32[256,16,64]{2,1,0:T(8,128)} fusion(bf16[256,16,256]{2,1,0:T(8,128)(2,1)S(1)} %get-tuple-element.14, bf16[256,64,256]{2,1,0:T(8,128)(2,1)} %bitcast.6), kind=kOutput, calls=%fused_computation.53 | convolution fusion | flops 134217728 | bytes 11534336 | tf_op jit(solution)/shard_map/pkd,pbd->pkb/dot_general | solution.py:27
  344.7 13.1 %psum.39 = f32[256,16]{1,0:T(8,128)S(1)} all-reduce(f32[256,16]{1,0:T(8,128)S(1)} %get-tuple-element.13), channel_id=1, replica_groups=mesh['dp'=64,'grp'=4] {'grp'}, use_global_device_ids=true, to_apply=%region_11.12 | all-reduce | flops 4096 | bytes 32768 | tf_op jit(solution)/shard_map/psum | solution.py:19
  357.9 50.7 %all-reduce.4.cloned.1.call-done = f32[256,16,64]{2,1,0:T(8,128)} async-done(((f32[256,16,64]{2,1,0:T(8,128)}), f32[256,16,64]{2,1,0:T(8,128)}) %all-reduce.4.cloned.1.call-update) | async-done | bytes 1048592 | tf_op jit(solution)/shard_map/psum | solution.py:19
  408.7 2.9 fusion.8
  411.6 1.7 convert_reduce_fusion
  413.3 4.8 %fusion.6 = bf16[256,16,256]{2,1,0:T(8,128)(2,1)S(1)} fusion(bf16[256,16,256]{2,1,0:T(8,128)(2,1)S(1)} %copy-done.4, bf16[256,16,64]{2,1,0:T(8,128)(2,1)S(1)} %get-tuple-element.8, bf16[256,64,256]{2,1,0:T(8,128)(2,1)} %bitcast.6, f32[256,16]{1,0:T(8,128)S(1)} %broadcast_add_fusion), kind=kOutput, calls=%fused_computation.16 | convolution fusion | flops 138412032 | bytes 13123584 | tf_op jit(solution)/shard_map/pkb,pbd->pkd/dot_general | solution.py:43
  418.1 1.0 broadcast_in_dim.36
  419.1 27.5 %scatter_fusion.3 = bf16[128,16,256]{2,1,0:T(8,128)(2,1)} fusion(bf16[128,16,256]{2,1,0:T(8,128)(2,1)} %broadcast_in_dim.36, s32[256]{0:T(256)S(1)} %bitcast.28, bf16[256,16,256]{2,1,0:T(8,128)(2,1)S(1)} %fusion.6), kind=kCustom, calls=%fused_computation.4 | custom fusion | bytes 6292480 | tf_op jit(solution)/shard_map/scatter | solution.py:79
  (36 shorter events, 2.2 us)
Async XLA Ops:
  6.5 58.4 %copy-start = (bf16[128,16,256]{2,1,0:T(8,128)(2,1)S(1)}, bf16[128,16,256]{2,1,0:T(8,128)(2,1)}, u32[]{:S(2)}) copy-start(bf16[128,16,256]{2,1,0:T(8,128)(2,1)} %param.7) | copy-start | bytes 3145732
  14.9 38.0 %all-to-all-start = ((s32[64,1,4]{2,1,0:T(1,128)}), s32[64,1,4]{2,1,0:T(1,128)S(1)}, u32[]{:S(2)}, u32[]{:S(2)}) async-start(s32[64,1,4]{2,1,0:T(1,128)} %copy.8), calls=%async_computation | async-start | bytes 65536 | tf_op jit(solution)/shard_map/all_to_all | solution.py:72
  52.9 196.3 %all-to-all-start.2 = ((bf16[64,4,64,256]{3,2,1,0:T(8,128)(2,1)}), bf16[64,4,64,256]{3,2,1,0:T(8,128)(2,1)}, u32[]{:S(2)}, u32[]{:S(2)}) async-start(bf16[64,4,64,256]{3,2,1,0:T(8,128)(2,1)} %scatter_fusion.2), calls=%async_computation.2 | async-start | bytes 16777216 | tf_op jit(solution)/shard_map/all_to_all | solution.py:70
  63.5 262.5 %all-reduce.6.cloned.1.call-start = ((), (), s32[]{:S(2)}) async-start(), calls=%async_computation.4 | async-start | bytes 4456448 | tf_op jit(solution)/shard_map/psum | solution.py:19
  262.5 0.7 copy-start.6
  262.5 146.1 %all-reduce.4.cloned.1.call-start = ((), (), s32[]{:S(2)}) async-start(), calls=%async_computation.3 | async-start | bytes 4194304 | tf_op jit(solution)/shard_map/psum | solution.py:19
  302.8 27.1 %copy-start.5 = (pred[256,64]{1,0:T(8,128)(4,1)S(1)}, pred[256,64]{1,0:T(8,128)(4,1)}, u32[]{:S(2)}) copy-start(pred[256,64]{1,0:T(8,128)(4,1)} %iota_compare_fusion) | copy-start | bytes 49156
  326.0 4.0 copy-start.1
  336.3 1.4 copy-start.3
  408.7 2.9 copy-start.2
  411.5 1.7 copy-start.4
Sparse Core Ops, SparseCore 0:
  262.7 63.2 all-reduce.5
  344.9 63.7 all-reduce.3
where the time goes:
time: 455 us; the launch traced here: 454 us
  waiting for transfers between devices  257 us (56%)
  local copies, waits for them, and re-layouts  70.9 us (16%)
  blocking collectives  43.1 us (9%)
  starting transfers between devices  23.6 us (5%)
  matrix products  23.5 us (5%)
  other arithmetic  21.4 us (5%)
  between operations  13.7 us (3%)
    all_to_all x1, waiting for transfers between devices, on_device(): lax.all_to_all(blocks, 'dp', split_axis=0, concat_axis=0, tiled=True)  184 us
    psum x2, waiting for transfers between devices, part_totals(): return lax.psum((cosine_similarity_matrix, centre_sq), 'grp')  73.9 us
    psum x2, blocking collectives, part_totals(): return lax.psum((cosine_similarity_matrix, centre_sq), 'grp')  28.2 us
    scatter x1, local copies, waits for them, and re-layouts, on_device(): jnp.zeros_like(centroids).at[flat_slots].set(updated_output, mode='drop')  27.5 us
    scatter x1, local copies, waits for them, and re-layouts, on_device(): blocks = jnp.zeros((peers, capacity, block_rows, width_part), jnp.bfloat1...  20.8 us
    all_to_all x1, blocking collectives, on_device(): lax.all_to_all(sizes, 'dp', split_axis=0, concat_axis=0, tiled=True)  14.9 us
    dot_general x2, matrix products, refine(): jnp.einsum('pkd,pbd->pkb', current, vectors, preferred_element_type=jnp.f...  14.1 us
    all_to_all x1, starting transfers between devices, on_device(): lax.all_to_all(slots, 'dp', split_axis=0, concat_axis=0, tiled=True)  13 us
  transfers between devices with their start and end apart: 4, of which 3 were waited for; matrix products, arithmetic and copies ran while one was open for 8% of the time, Pallas kernels for 0%

commit v1 on v0

v1 whole, which is shorter than its diff:
```python
import functools

import jax
import jax.numpy as jnp
from jax import lax
from jax.experimental import pallas as pl
from jax.experimental.pallas import tpu as pltpu
from jax.sharding import PartitionSpec as P

ITERS = 2
CAP = 4
LANES = 128

sharpness = 0.02
prior = 1.0
epsilon = 1e-06

MESH = pl.DeviceIdType.MESH


def wait_bytes(ref, sem):
    pltpu.make_async_copy(ref, ref, sem).wait()


def dot_t(left, right):
    return lax.dot_general(
        left, right, (((1,), (1,)), ((), ())), preferred_element_type=jnp.float32
    )


def kernel(
    n, groups, stride,
    msg, meta, posmap, x_hbm, cent_hbm,
    out, slots_out,
    x, cent, slotrecv, slot_s, c0send, c0recv, start, osend, cur,
    ysend, yrecv, wbuf, rsend, rrecv, rscale,
    load_sem, slot_send, slot_recv, c0_send, c0_recv, o_send, o_recv, own_sem,
    r_send, r_recv, y_send, y_recv, w_send, w_recv,
):
    parents, block, width = x.shape
    children = cent.shape[1]
    chunk = parents // CAP
    per_owner = chunk // 2 // groups
    me = lax.axis_index("dp")
    g = lax.axis_index("grp")

    def peer(i):
        return lax.rem(me + lax.rem(i * stride, n), n)

    def mate(i):
        return lax.rem(g + i, groups)

    load_x = pltpu.make_async_copy(x_hbm, x, load_sem.at[0])
    load_c = pltpu.make_async_copy(cent_hbm, cent, load_sem.at[1])
    load_c.start()
    load_x.start()

    barrier = pltpu.get_barrier_semaphore()

    @pl.loop(1, n)
    def _(i):
        pl.semaphore_signal(barrier, inc=1, device_id=(peer(i), g), device_id_type=MESH)

    @pl.loop(1, groups)
    def _(i):
        pl.semaphore_signal(barrier, inc=1, device_id=(me, mate(i)), device_id_type=MESH)

    pl.semaphore_wait(barrier, n - 1 + groups - 1)

    @pl.loop(1, n)
    def _(i):
        p = peer(i)
        pltpu.make_async_remote_copy(
            src_ref=msg.at[p], dst_ref=slotrecv.at[me],
            send_sem=slot_send, recv_sem=slot_recv,
            device_id=(p, g), device_id_type=MESH,
        ).start()

    slotrecv[me] = msg[me]
    load_c.wait()
    wait_bytes(slotrecv.at[pl.ds(0, n - 1)], slot_recv)
    to_scalars = pltpu.make_async_copy(slotrecv, slot_s, load_sem.at[2])
    to_scalars.start()
    to_scalars.wait()

    @pl.loop(0, CAP)
    def _(j):
        @pl.loop(0, n)
        def _(h):
            slot = jnp.minimum(slot_s[h, 0, j], parents - 1)
            c0send[j, h] = cent[slot]

        c0recv[j, me] = c0send[j, me]

        @pl.loop(1, n)
        def _(i):
            p = peer(i)
            pltpu.make_async_remote_copy(
                src_ref=c0send.at[j, p], dst_ref=c0recv.at[j, me],
                send_sem=c0_send.at[j], recv_sem=c0_recv.at[j],
                device_id=(p, g), device_id_type=MESH,
            ).start()

    slots_out[...] = slotrecv[...]

    lane = lax.broadcasted_iota(jnp.int32, (children, LANES), 1)
    first = lane < block
    load_x.wait()

    def rows_of(j, index):
        at = j * chunk + 2 * index
        return jnp.concatenate([x[meta[0, at]], x[meta[0, at + 1]]], axis=0)

    eye = lax.broadcasted_iota(jnp.int32, (LANES, LANES), 0) == lax.broadcasted_iota(
        jnp.int32, (LANES, LANES), 1
    )

    @pl.loop(0, CAP)
    def _(j):
        @pl.loop(0, groups)
        def _(o):
            for q in range(per_owner):
                rows = rows_of(j, o * per_owner + q)
                gram = dot_t(rows, rows)
                rsend[o, pl.ds(j * per_owner + q, 1), :] = jnp.sum(
                    jnp.where(eye, gram, 0.0), axis=0, keepdims=True
                )

    @pl.loop(1, groups)
    def _(i):
        o = mate(i)
        pltpu.make_async_remote_copy(
            src_ref=rsend.at[o], dst_ref=rrecv.at[g],
            send_sem=r_send, recv_sem=r_recv,
            device_id=(me, o), device_id_type=MESH,
        ).start()

    wait_bytes(rrecv.at[pl.ds(0, groups - 1)], r_recv)
    row_sq = rsend[g]
    for i in range(1, groups):
        row_sq += rrecv[mate(i)]
    rscale[...] = lax.rsqrt(row_sq + epsilon)

    def updated(j, t, o, q, rows):
        at = 2 * (o * per_owner + q)
        old = jnp.concatenate([cur[at], cur[at + 1]], axis=0).astype(jnp.float32)
        weights = wbuf[j, t, o, q].astype(jnp.float32)
        both = jnp.concatenate(
            [jnp.where(first, weights, 0.0), jnp.where(first, 0.0, weights)], axis=0
        )
        moments = jnp.dot(both.astype(jnp.bfloat16), rows, preferred_element_type=jnp.float32)
        totals = jnp.sum(both, axis=1, keepdims=True)
        return ((moments + prior * old) * (1.0 / (totals + prior))).astype(jnp.bfloat16)

    def keep(o, q, both):
        at = 2 * (o * per_owner + q)
        cur[at] = both[:children]
        cur[at + 1] = both[children:]

    @pl.loop(0, CAP)
    def _(j):
        wait_bytes(c0recv.at[j, pl.ds(0, n - 1)], c0_recv.at[j])

        @pl.loop(0, n)
        def _(h):
            start[h] = c0recv[j, h]

        for t in range(ITERS):

            def send_scores(i):
                o = mate(i)
                pltpu.make_async_remote_copy(
                    src_ref=ysend.at[j, t, o], dst_ref=yrecv.at[j, t, g],
                    send_sem=y_send.at[j, t], recv_sem=y_recv.at[j, t],
                    device_id=(me, o), device_id_type=MESH,
                ).start()

            @pl.loop(1, groups + 1)
            def _(i):
                @pl.when(i > 1)
                def _():
                    send_scores(i - 1)

                o = mate(i)
                centre_sq = jnp.zeros((children, LANES), jnp.float32)
                for q in range(per_owner):
                    index = o * per_owner + q
                    rows = rows_of(j, index)
                    if t == 0:
                        at = j * chunk + 2 * index
                        both = jnp.concatenate(
                            [start[meta[1, at]], start[meta[1, at + 1]]], axis=0
                        )
                    else:
                        both = updated(j, t - 1, o, q, rows)
                    keep(o, q, both)
                    part = dot_t(both, rows)
                    ysend[j, t, o, q] = jnp.where(first, part[:children], part[children:])
                    wide = both.astype(jnp.float32)
                    sq = jnp.sum(wide * wide, axis=1, keepdims=True)
                    centre_sq = jnp.where(lane == 2 * q, sq[:children], centre_sq)
                    centre_sq = jnp.where(lane == 2 * q + 1, sq[children:], centre_sq)
                ysend[j, t, o, per_owner] = centre_sq

            wait_bytes(yrecv.at[j, t, pl.ds(0, groups - 1)], y_recv.at[j, t])

            def total(q):
                value = ysend[j, t, g, q]
                for i in range(1, groups):
                    value += yrecv[j, t, mate(i), q]
                return value

            centre_scale = lax.rsqrt(total(per_owner) + epsilon)
            for q in range(per_owner):
                at = j * chunk + 2 * (g * per_owner + q)
                centres = jnp.where(
                    first, centre_scale[:, 2 * q : 2 * q + 1], centre_scale[:, 2 * q + 1 : 2 * q + 2]
                )
                scores = (
                    total(q) * centres * rscale[pl.ds(j * per_owner + q, 1), :] * (1.0 / sharpness)
                )
                raised = jnp.exp(scores)
                share = raised * (1.0 / jnp.sum(raised, axis=0, keepdims=True))
                live = lane < jnp.where(first, meta[2, at], meta[2, at + 1] + block)
                wbuf[j, t, g, q] = jnp.where(live, share, 0.0).astype(jnp.bfloat16)

            wait_bytes(ysend.at[j, t, pl.ds(0, groups - 1)], y_send.at[j, t])

            @pl.loop(1, groups)
            def _(i):
                pltpu.make_async_remote_copy(
                    src_ref=wbuf.at[j, t, g], dst_ref=wbuf.at[j, t, g],
                    send_sem=w_send.at[j, t], recv_sem=w_recv.at[j, t],
                    device_id=(me, mate(i)), device_id_type=MESH,
                ).start()

            wait_bytes(wbuf.at[j, t, pl.ds(0, groups - 1)], w_recv.at[j, t])

        @pl.loop(0, groups)
        def _(o):
            for q in range(per_owner):
                keep(o, q, updated(j, ITERS - 1, o, q, rows_of(j, o * per_owner + q)))

        @pl.loop(0, n)
        def _(h):
            osend[j, h] = cur[posmap[j, h]]

        @pl.loop(1, n)
        def _(i):
            p = peer(i)
            pltpu.make_async_remote_copy(
                src_ref=osend.at[j, p], dst_ref=out.at[j, me],
                send_sem=o_send.at[j], recv_sem=o_recv.at[j],
                device_id=(p, g), device_id_type=MESH,
            ).start()

        pltpu.make_async_copy(osend.at[j, me], out.at[j, me], own_sem.at[j]).start()

    wait_bytes(msg.at[pl.ds(0, n - 1)], slot_send)
    wait_bytes(rsend.at[pl.ds(0, groups - 1)], r_send)

    @pl.loop(0, CAP)
    def _(j):
        wait_bytes(c0send.at[j, pl.ds(0, n - 1)], c0_send.at[j])
        for t in range(ITERS):
            wait_bytes(wbuf.at[j, t, pl.ds(0, groups - 1)], w_send.at[j, t])
        wait_bytes(osend.at[j, pl.ds(0, n - 1)], o_send.at[j])
        pltpu.make_async_copy(osend.at[j, me], out.at[j, me], own_sem.at[j]).wait()
        wait_bytes(out.at[j, pl.ds(0, n - 1)], o_recv.at[j])


def on_device(embeddings, lengths, parent_slot, centroids):
    parents, block, width = embeddings.shape
    children = centroids.shape[1]
    n = lax.axis_size("dp")
    groups = lax.axis_size("grp")
    chunk = parents // CAP
    per_owner = chunk // 2 // groups
    stride = 27 if n % 27 else 1

    holder = parent_slot // parents
    local = parent_slot - holder * parents
    ids = jnp.arange(parents, dtype=jnp.int32)
    earlier = ids[None, :] < ids[:, None]
    order = jnp.sum((earlier & (holder[None, :] == holder[:, None])).astype(jnp.int32), axis=1)
    within = jnp.sum((earlier & (order[None, :] == order[:, None])).astype(jnp.int32), axis=1)
    place = order * chunk + within
    at_place = (place[None, :] == ids[:, None]).astype(jnp.int32)
    meta = jnp.sum(at_place[None] * jnp.stack([ids, holder, lengths])[:, None, :], axis=2)
    cells = jnp.arange(CAP * n, dtype=jnp.int32)
    at_cell = ((order * n + holder)[None, :] == cells[:, None]).astype(jnp.int32)
    posmap = jnp.sum(at_cell * within[None, :], axis=1).reshape(CAP, n)
    asked = jnp.sum(at_cell * (local - parents)[None, :], axis=1).reshape(CAP, n) + parents
    msg = jnp.pad(asked.T, ((0, 0), (0, LANES - CAP)))[:, None, :]

    dma = pltpu.SemaphoreType.DMA
    cell_block = (CAP, n, children, width)
    vmem, smem = pltpu.VMEM, pltpu.SMEM
    out, slots = pl.pallas_call(
        functools.partial(kernel, n, groups, stride),
        out_shape=(
            jax.ShapeDtypeStruct(cell_block, jnp.bfloat16),
            jax.ShapeDtypeStruct((n, 1, LANES), jnp.int32),
        ),
        in_specs=[
            pl.BlockSpec(memory_space=vmem),
            pl.BlockSpec(memory_space=smem),
            pl.BlockSpec(memory_space=smem),
            pl.BlockSpec(memory_space=pl.ANY),
            pl.BlockSpec(memory_space=pl.ANY),
        ],
        out_specs=(pl.BlockSpec(memory_space=pl.ANY), pl.BlockSpec(memory_space=vmem)),
        scratch_shapes=[
            vmem((parents, block, width), jnp.bfloat16),
            vmem((parents, children, width), jnp.bfloat16),
            vmem((n, 1, LANES), jnp.int32),
            smem((n, 1, LANES), jnp.int32),
            vmem(cell_block, jnp.bfloat16),
            vmem(cell_block, jnp.bfloat16),
            vmem(cell_block[1:], jnp.bfloat16),
            vmem(cell_block, jnp.bfloat16),
            vmem((chunk, children, width), jnp.bfloat16),
            vmem((CAP, ITERS, groups, per_owner + 1, children, LANES), jnp.float32),
            vmem((CAP, ITERS, groups, per_owner + 1, children, LANES), jnp.float32),
            vmem((CAP, ITERS, groups, per_owner, children, LANES), jnp.bfloat16),
            vmem((groups, CAP * per_owner, LANES), jnp.float32),
            vmem((groups, CAP * per_owner, LANES), jnp.float32),
            vmem((CAP * per_owner, LANES), jnp.float32),
            dma((3,)),
            dma, dma,
            dma((CAP,)), dma((CAP,)), dma((CAP,)), dma((CAP,)), dma((CAP,)),
            dma, dma,
            dma((CAP, ITERS)), dma((CAP, ITERS)), dma((CAP, ITERS)), dma((CAP, ITERS)),
        ],
        compiler_params=pltpu.CompilerParams(collective_id=0, has_side_effects=True),
        name="refine",
    )(msg, meta, posmap, embeddings, centroids)

    asked_here = slots[:, 0, :CAP].T.reshape(1, CAP * n)
    source = jnp.sum(
        (asked_here == ids[:, None]).astype(jnp.int32) * cells[None, :], axis=1
    )
    rows = out.reshape(CAP * n, children, width)
    return rows.at[source].get(mode="promise_in_bounds")


def solution(mesh):
    return jax.shard_map(
        on_device,
        mesh=mesh,
        in_specs=(P("dp", None, "grp"), P("dp"), P("dp"), P("dp", None, "grp")),
        out_specs=P("dp", None, "grp"),
        check_vma=False,
    )
```

time: 455 us -> 135 us (0.30)
  waiting for transfers between devices: 257 us -> 0 us
  Pallas kernels: 0 us -> 127 us
  local copies, waits for them, and re-layouts: 70.9 us -> 5.59 us
  blocking collectives: 43.1 us -> 0 us
  starting transfers between devices: 23.6 us -> 0 us
  matrix products: 23.5 us -> 0 us
  other arithmetic: 21.4 us -> 2.72 us
  between operations: 13.7 us -> 0.05 us
    all_to_all x2 -> x0, waiting for transfers between devices: 184 us -> none  [the longest x1 184 us: on_device(): lax.all_to_all(blocks, 'dp', split_axis=0, concat_axis=0, tiled=True)]
    pallas_call x0 -> x1, Pallas kernels: none -> 127 us  [on_device(): pl.pallas_call(functools.partial(kernel, n, groups, stride), out_shape=(j...]
    psum x2 -> x0, waiting for transfers between devices: 73.9 us -> none  [part_totals(): return lax.psum((cosine_similarity_matrix, centre_sq), 'grp')]
    scatter x4 -> x0, local copies, waits for them, and re-layouts: 61.2 us -> none  [the longest x1 27.5 us: on_device(): jnp.zeros_like(centroids).at[flat_slots].set(updated_output, mode='drop')]
    psum x2 -> x0, blocking collectives: 28.2 us -> none  [part_totals(): return lax.psum((cosine_similarity_matrix, centre_sq), 'grp')]
    all_to_all x2 -> x0, starting transfers between devices: 23.5 us -> none  [the longest x1 13 us: on_device(): lax.all_to_all(slots, 'dp', split_axis=0, concat_axis=0, tiled=True)]
    dot_general x4 -> x0, matrix products: 23.5 us -> none  [the longest x2 14.1 us: refine(): jnp.einsum('pkd,pbd->pkb', current, vectors, preferred_element_type=jnp.f...]
    all_to_all x1 -> x0, blocking collectives: 14.9 us -> none  [on_device(): lax.all_to_all(sizes, 'dp', split_axis=0, concat_axis=0, tiled=True)]
  transfers between devices with their start and end apart: 4 -> 0, of which waited for: 3 -> 0; matrix products, arithmetic and copies ran while one was open for 8% -> 0% of each run, Pallas kernels for 0% -> 0%
where the time goes in v1:
time: 135 us
  Pallas kernels  127 us (94%)
  local copies, waits for them, and re-layouts  5.59 us (4%)
  other arithmetic  2.72 us (2%)
    pallas_call x1, Pallas kernels, on_device(): pl.pallas_call(functools.partial(kernel, n, groups, stride), out_shape=(j...  127 us
    gather x1, local copies, waits for them, and re-layouts, on_device(): return rows.at[source].get(mode='promise_in_bounds')  3.2 us

profile of v1, /device:TPU:1, one launch (start us, length us, event | category | flops | bytes accessed | tf_op | source)
XLA Modules:
  0.0 135.0 jit_solution(15558549520006360779)
XLA Ops:
  0.0 0.7 subtract_add_fusion
  0.7 0.2 convert_reduce_fusion.1
  0.8 0.2 convert_reduce_fusion
  1.0 0.2 select_reduce_fusion.1
  1.2 0.7 reshape.59.posmap
  1.9 0.1 add.39
  2.0 0.7 pad_add_fusion
  2.6 0.1 copy.7
  2.7 0.6 pad.4
  3.4 0.7 multiply_reduce_fusion.meta
  4.1 126.7 %refine.1 = (bf16[4,64,16,256]{3,2,1,0:T(8,128)(2,1)}, s32[64,1,128]{2,1,0:T(1,128)}) custom-call(s32[64,1,128]{2,1,0:T(1,128)} %bitcast.14, s32[3,128]{1,0:T(4,128)} %multiply_reduce_fusion.meta, s32[4,64]{1,0:T(4,128)} %reshape.59.posmap, bf16[128,64,256]{2,1,0:T(8,128)(2,1)} %x_hbm.1, bf16[128,16,256]{2,1,0:T(8,128)(2,1)} %cent_hbm.1), custom_call_target="tpu_custom_call" | custom-call | tf_op jit(solution)/shard_map/refine/pallas_call | solution.py:299
  130.8 0.8 copy.8
  131.6 0.1 eq.80
  131.7 0.1 select_reduce_fusion
  131.8 3.2 %gather_fusion = bf16[128,16,256]{2,1,0:T(8,128)(2,1)} fusion(bf16[256,16,256]{2,1,0:T(8,128)(2,1)} %bitcast.13, s32[1024]{0:T(1024)S(1)} %pad_clamp_fusion), kind=kCustom, calls=%fused_computation | custom fusion | bytes 2097664 | tf_op jit(solution)/shard_map/gather | solution.py:344
  (6 shorter events, 0.0 us)

commit v2 on v1

v2 whole, which is shorter than its diff:
```python
import functools

import jax
import jax.numpy as jnp
from jax import lax
from jax.experimental import pallas as pl
from jax.experimental.pallas import tpu as pltpu
from jax.sharding import PartitionSpec as P

ITERS = 2
CAP = 4
LANES = 128

sharpness = 0.02
prior = 1.0
epsilon = 1e-06

MESH = pl.DeviceIdType.MESH


def wait_bytes(ref, sem):
    pltpu.make_async_copy(ref, ref, sem).wait()


def dot_t(left, right):
    return lax.dot_general(
        left, right, (((1,), (1,)), ((), ())), preferred_element_type=jnp.float32
    )


def kernel(
    n, groups, stride,
    slot_hbm, length_hbm, x_hbm, cent_hbm,
    refined,
    slot_v, length_v, msg_flat, msg, meta_v, meta, inverse_v, inverse,
    x, cent, slotrecv, slot_s, c0send, c0recv, start, osend, orecv, cur,
    ysend, yrecv, wbuf, rsend, rrecv, rscale,
    load_sem, slot_send, slot_recv, c0_send, c0_recv, o_send, o_recv,
    r_send, r_recv, y_send, y_recv, w_send, w_recv,
):
    parents, block, width = x.shape
    children = cent.shape[1]
    chunk = parents // CAP
    per_owner = chunk // 2 // groups
    me = lax.axis_index("dp")
    g = lax.axis_index("grp")

    def peer(i):
        return lax.rem(me + lax.rem(i * stride, n), n)

    def mate(i):
        return lax.rem(g + i, groups)

    def load(source, target, k):
        copy = pltpu.make_async_copy(source, target, load_sem.at[k])
        copy.start()
        return copy

    load_slot = load(slot_hbm, slot_v, 0)
    load_length = load(length_hbm, length_v, 1)

    barrier = pltpu.get_barrier_semaphore()

    @pl.loop(1, n)
    def _(i):
        pl.semaphore_signal(barrier, inc=1, device_id=(peer(i), g), device_id_type=MESH)

    @pl.loop(1, groups)
    def _(i):
        pl.semaphore_signal(barrier, inc=1, device_id=(me, mate(i)), device_id_type=MESH)

    load_c = load(cent_hbm, cent, 2)
    load_x = load(x_hbm, x, 3)
    load_slot.wait()
    load_length.wait()

    def iota(shape, dim):
        return lax.broadcasted_iota(jnp.int32, shape, dim)

    square = (parents, parents)
    sub, lan = iota(square, 0), iota(square, 1)

    def column(row):
        return jnp.sum(jnp.where(sub == lan, row, 0), axis=1, keepdims=True)

    def count(mask, axis):
        return jnp.sum(jnp.where(mask, 1, 0), axis=axis, keepdims=True)

    bits = parents.bit_length() - 1
    slot_row = slot_v[...]
    holder_row = lax.shift_right_logical(slot_row, bits)
    local_row = slot_row - lax.shift_left(holder_row, bits)
    holder = column(holder_row)
    same = holder == holder_row
    order_row = count(same & (sub < lan), 0)
    order = count(same & (lan < sub), 1)

    asked = jnp.zeros((n, LANES), jnp.int32)
    for j in range(CAP):
        hit = (holder_row == iota((n, parents), 0)) & (order_row == j)
        slot_j = jnp.sum(jnp.where(hit, local_row - parents, 0), axis=1, keepdims=True) + parents
        asked = jnp.where(iota((n, LANES), 1) == j, slot_j, asked)
    msg_flat[...] = asked

    @pl.loop(0, n)
    def _(h):
        msg[h] = msg_flat[pl.ds(h, 1), :]

    slotrecv[me] = msg[me]

    within = count((order == order_row) & (lan < sub), 1)
    hit = order * chunk + within == lan
    for k, value in enumerate((sub, holder, column(length_v[...]))):
        meta_v[k] = jnp.sum(jnp.where(hit, value, 0), axis=0, keepdims=True)
    for j in range(CAP):
        hit = (holder == lan) & (order == j)
        meta_v[3 + j] = jnp.sum(jnp.where(hit, within, 0), axis=0, keepdims=True)
    to_meta = load(meta_v, meta, 4)

    pl.semaphore_wait(barrier, n - 1 + groups - 1)

    @pl.loop(1, n)
    def _(i):
        p = peer(i)
        pltpu.make_async_remote_copy(
            src_ref=msg.at[p], dst_ref=slotrecv.at[me],
            send_sem=slot_send, recv_sem=slot_recv,
            device_id=(p, g), device_id_type=MESH,
        ).start()

    load_c.wait()
    to_meta.wait()
    wait_bytes(slotrecv.at[pl.ds(0, n - 1)], slot_recv)
    to_scalars = load(slotrecv, slot_s, 5)
    to_scalars.wait()

    @pl.loop(0, CAP)
    def _(j):
        @pl.loop(0, n, step=4)
        def _(h):
            for k in range(4):
                slot = jnp.minimum(slot_s[h + k, 0, j], parents - 1)
                c0send[j, h + k] = cent[slot]

        c0recv[j, me] = c0send[j, me]

        @pl.loop(1, n)
        def _(i):
            p = peer(i)
            pltpu.make_async_remote_copy(
                src_ref=c0send.at[j, p], dst_ref=c0recv.at[j, me],
                send_sem=c0_send.at[j], recv_sem=c0_recv.at[j],
                device_id=(p, g), device_id_type=MESH,
            ).start()

    row = iota((1, parents), 1)

    def note(s, found):
        for j in range(CAP):
            found = jnp.where(row == slot_s[s, 0, j], j * n + s, found)
        return found

    inverse_v[0] = lax.fori_loop(0, n, note, jnp.zeros((1, parents), jnp.int32))
    to_inverse = load(inverse_v, inverse, 6)

    lane = iota((children, LANES), 1)
    first = lane < block
    load_x.wait()

    def rows_of(j, index):
        at = j * chunk + 2 * index
        return jnp.concatenate([x[meta[0, 0, at]], x[meta[0, 0, at + 1]]], axis=0)

    eye = iota((LANES, LANES), 0) == iota((LANES, LANES), 1)

    @pl.loop(0, CAP)
    def _(j):
        @pl.loop(0, groups)
        def _(o):
            for q in range(per_owner):
                rows = rows_of(j, o * per_owner + q)
                gram = dot_t(rows, rows)
                rsend[o, pl.ds(j * per_owner + q, 1), :] = jnp.sum(
                    jnp.where(eye, gram, 0.0), axis=0, keepdims=True
                )

    @pl.loop(1, groups)
    def _(i):
        o = mate(i)
        pltpu.make_async_remote_copy(
            src_ref=rsend.at[o], dst_ref=rrecv.at[g],
            send_sem=r_send, recv_sem=r_recv,
            device_id=(me, o), device_id_type=MESH,
        ).start()

    to_inverse.wait()
    wait_bytes(rrecv.at[pl.ds(0, groups - 1)], r_recv)
    row_sq = rsend[g]
    for i in range(1, groups):
        row_sq += rrecv[mate(i)]
    rscale[...] = lax.rsqrt(row_sq + epsilon)

    def place(j, o, q):
        return lax.rem(j, 2) * chunk + 2 * (o * per_owner + q)

    def updated(j, t, o, q, rows):
        at = place(j, o, q)
        old = jnp.concatenate([cur[at], cur[at + 1]], axis=0).astype(jnp.float32)
        weights = wbuf[j, t, o, q].astype(jnp.float32)
        both = jnp.concatenate(
            [jnp.where(first, weights, 0.0), jnp.where(first, 0.0, weights)], axis=0
        )
        moments = jnp.dot(both.astype(jnp.bfloat16), rows, preferred_element_type=jnp.float32)
        totals = jnp.sum(both, axis=1, keepdims=True)
        return ((moments + prior * old) * (1.0 / (totals + prior))).astype(jnp.bfloat16)

    def keep(j, o, q, both):
        at = place(j, o, q)
        cur[at] = both[:children]
        cur[at + 1] = both[children:]

    def send_scores(j, t):
        def send(i):
            o = mate(i)
            pltpu.make_async_remote_copy(
                src_ref=ysend.at[j, t, o], dst_ref=yrecv.at[j, t, g],
                send_sem=y_send.at[j, t], recv_sem=y_recv.at[j, t],
                device_id=(me, o), device_id_type=MESH,
            ).start()

        @pl.loop(1, groups + 1)
        def _(i):
            @pl.when(i > 1)
            def _():
                send(i - 1)

            o = mate(i)
            centre_sq = jnp.zeros((children, LANES), jnp.float32)
            for q in range(per_owner):
                index = o * per_owner + q
                rows = rows_of(j, index)
                if t == 0:
                    at = j * chunk + 2 * index
                    both = jnp.concatenate(
                        [start[meta[1, 0, at]], start[meta[1, 0, at + 1]]], axis=0
                    )
                else:
                    both = updated(j, t - 1, o, q, rows)
                keep(j, o, q, both)
                part = dot_t(both, rows)
                ysend[j, t, o, q] = jnp.where(first, part[:children], part[children:])
                wide = both.astype(jnp.float32)
                sq = jnp.sum(wide * wide, axis=1, keepdims=True)
                centre_sq = jnp.where(lane == 2 * q, sq[:children], centre_sq)
                centre_sq = jnp.where(lane == 2 * q + 1, sq[children:], centre_sq)
            ysend[j, t, o, per_owner] = centre_sq

    def begin(j):
        wait_bytes(c0recv.at[j, pl.ds(0, n - 1)], c0_recv.at[j])

        @pl.loop(0, n, step=4)
        def _(h):
            for k in range(4):
                start[h + k] = c0recv[j, h + k]

        send_scores(j, 0)

    def weigh(j, t):
        wait_bytes(yrecv.at[j, t, pl.ds(0, groups - 1)], y_recv.at[j, t])

        def total(q):
            value = ysend[j, t, g, q]
            for i in range(1, groups):
                value += yrecv[j, t, mate(i), q]
            return value

        centre_scale = lax.rsqrt(total(per_owner) + epsilon)
        for q in range(per_owner):
            at = j * chunk + 2 * (g * per_owner + q)
            centres = jnp.where(
                first, centre_scale[:, 2 * q : 2 * q + 1], centre_scale[:, 2 * q + 1 : 2 * q + 2]
            )
            scores = (
                total(q) * centres * rscale[pl.ds(j * per_owner + q, 1), :] * (1.0 / sharpness)
            )
            raised = jnp.exp(scores)
            share = raised * (1.0 / jnp.sum(raised, axis=0, keepdims=True))
            live = lane < jnp.where(first, meta[2, 0, at], meta[2, 0, at + 1] + block)
            wbuf[j, t, g, q] = jnp.where(live, share, 0.0).astype(jnp.bfloat16)

        wait_bytes(ysend.at[j, t, pl.ds(0, groups - 1)], y_send.at[j, t])

        @pl.loop(1, groups)
        def _(i):
            pltpu.make_async_remote_copy(
                src_ref=wbuf.at[j, t, g], dst_ref=wbuf.at[j, t, g],
                send_sem=w_send.at[j, t], recv_sem=w_recv.at[j, t],
                device_id=(me, mate(i)), device_id_type=MESH,
            ).start()

    def weights_here(j, t):
        wait_bytes(wbuf.at[j, t, pl.ds(0, groups - 1)], w_recv.at[j, t])

    def step_again(j):
        weights_here(j, 0)
        send_scores(j, 1)

    def finish(j):
        weights_here(j, ITERS - 1)

        @pl.loop(0, groups)
        def _(o):
            for q in range(per_owner):
                keep(j, o, q, updated(j, ITERS - 1, o, q, rows_of(j, o * per_owner + q)))

        base = lax.rem(j, 2) * chunk

        @pl.loop(0, n, step=4)
        def _(h):
            for k in range(4):
                osend[j, h + k] = cur[base + meta[3 + j, 0, h + k]]

        orecv[j * n + me] = osend[j, me]

        @pl.loop(1, n)
        def _(i):
            p = peer(i)
            pltpu.make_async_remote_copy(
                src_ref=osend.at[j, p], dst_ref=orecv.at[j * n + me],
                send_sem=o_send.at[j], recv_sem=o_recv.at[j],
                device_id=(p, g), device_id_type=MESH,
            ).start()

    begin(0)
    weigh(0, 0)
    step_again(0)

    @pl.loop(1, CAP)
    def _(j):
        begin(j)
        weigh(j - 1, 1)
        weigh(j, 0)
        finish(j - 1)
        step_again(j)

    weigh(CAP - 1, 1)
    finish(CAP - 1)

    wait_bytes(msg.at[pl.ds(0, n - 1)], slot_send)
    wait_bytes(rsend.at[pl.ds(0, groups - 1)], r_send)

    @pl.loop(0, CAP)
    def _(j):
        wait_bytes(c0send.at[j, pl.ds(0, n - 1)], c0_send.at[j])
        for t in range(ITERS):
            wait_bytes(wbuf.at[j, t, pl.ds(0, groups - 1)], w_send.at[j, t])
        wait_bytes(osend.at[j, pl.ds(0, n - 1)], o_send.at[j])
        wait_bytes(orecv.at[pl.ds(0, n - 1)], o_recv.at[j])

    @pl.loop(0, parents, step=8)
    def _(l):
        for k in range(8):
            refined[l + k] = orecv[inverse[0, 0, l + k]]


def on_device(embeddings, lengths, parent_slot, centroids):
    parents, block, width = embeddings.shape
    children = centroids.shape[1]
    n = lax.axis_size("dp")
    groups = lax.axis_size("grp")
    chunk = parents // CAP
    per_owner = chunk // 2 // groups
    stride = 27 if n % 27 else 1

    dma = pltpu.SemaphoreType.DMA
    vmem, smem = pltpu.VMEM, pltpu.SMEM
    cells = (CAP, n, children, width)
    ints = (n, 1, LANES)
    bf16, f32, i32 = jnp.bfloat16, jnp.float32, jnp.int32
    by_owner = (CAP, ITERS, groups, per_owner + 1, children, LANES)
    return pl.pallas_call(
        functools.partial(kernel, n, groups, stride),
        out_shape=jax.ShapeDtypeStruct(centroids.shape, bf16),
        in_specs=[pl.BlockSpec(memory_space=pl.ANY)] * 4,
        out_specs=pl.BlockSpec(memory_space=vmem),
        scratch_shapes=[
            vmem((1, parents), i32),
            vmem((1, parents), i32),
            vmem((n, LANES), i32),
            vmem(ints, i32),
            vmem((3 + CAP, 1, parents), i32),
            smem((3 + CAP, 1, parents), i32),
            vmem((1, 1, parents), i32),
            smem((1, 1, parents), i32),
            vmem((parents, block, width), bf16),
            vmem((parents, children, width), bf16),
            vmem(ints, i32),
            smem(ints, i32),
            vmem(cells, bf16),
            vmem(cells, bf16),
            vmem(cells[1:], bf16),
            vmem(cells, bf16),
            vmem((CAP * n, children, width), bf16),
            vmem((2 * chunk, children, width), bf16),
            vmem(by_owner, f32),
            vmem(by_owner, f32),
            vmem((CAP, ITERS, groups, per_owner, children, LANES), bf16),
            vmem((groups, CAP * per_owner, LANES), f32),
            vmem((groups, CAP * per_owner, LANES), f32),
            vmem((CAP * per_owner, LANES), f32),
            dma((7,)),
            dma, dma,
            dma((CAP,)), dma((CAP,)), dma((CAP,)), dma((CAP,)),
            dma, dma,
            dma((CAP, ITERS)), dma((CAP, ITERS)), dma((CAP, ITERS)), dma((CAP, ITERS)),
        ],
        compiler_params=pltpu.CompilerParams(collective_id=0, has_side_effects=True),
        name="refine",
    )(parent_slot.reshape(1, parents), lengths.reshape(1, parents), embeddings, centroids)


def solution(mesh):
    return jax.shard_map(
        on_device,
        mesh=mesh,
        in_specs=(P("dp", None, "grp"), P("dp"), P("dp"), P("dp", None, "grp")),
        out_specs=P("dp", None, "grp"),
        check_vma=False,
    )
```

time: 135 us -> 115 us (0.85)
  Pallas kernels: 127 us -> 113 us
  local copies, waits for them, and re-layouts: 5.59 us -> 2.26 us
  other arithmetic: 2.72 us -> 0 us
    pallas_call x1, Pallas kernels: 127 us -> 113 us  [on_device(): pl.pallas_call(functools.partial(kernel, n, groups, stride), out_shape=ja...]
    gather x1 -> x0, local copies, waits for them, and re-layouts: 3.2 us -> none  [on_device(): return rows.at[source].get(mode='promise_in_bounds')]
    unnamed x0 -> x1, local copies, waits for them, and re-layouts: none -> 2.26 us
    reduce_sum x5 -> x0, other arithmetic: 1.37 us -> none  [the longest x1 0.74 us: on_device(): jnp.sum(at_place[None] * jnp.stack([ids, holder, lengths])[:, None, :], a...]
where the time goes in v2:
time: 115 us
  Pallas kernels  113 us (98%)
  local copies, waits for them, and re-layouts  2.26 us (2%)
    pallas_call x1, Pallas kernels, on_device(): pl.pallas_call(functools.partial(kernel, n, groups, stride), out_shape=ja...  113 us

profile of v2, /device:TPU:1, one launch (start us, length us, event | category | flops | bytes accessed | tf_op | source)
XLA Modules:
  0.0 115.0 jit_solution(18241953950100974993)
XLA Ops:
  0.0 112.7 %refine.1 = bf16[128,16,256]{2,1,0:T(8,128)(2,1)} custom-call(s32[1,128]{1,0:T(1,128)} %bitcast.2, s32[1,128]{1,0:T(1,128)} %bitcast.3, bf16[128,64,256]{2,1,0:T(8,128)(2,1)} %x_hbm.1, bf16[128,16,256]{2,1,0:T(8,128)(2,1)} %cent_hbm.1), custom_call_target="tpu_custom_call" | custom-call | tf_op jit(solution)/shard_map/refine/pallas_call | solution.py:381
  112.7 2.3 %copy.6 = bf16[128,16,256]{2,1,0:T(8,128)(2,1)} copy(bf16[128,16,256]{2,1,0:T(8,128)(2,1)} %refine.1) | data formatting | bytes 2097152

commit v3 on v2

--- a/solution.py
+++ b/solution.py
@@ -29,13 +29,13 @@
 
 
 def kernel(
-    n, groups, stride,
+    n, groups, shape,
     slot_hbm, length_hbm, x_hbm, cent_hbm,
     refined,
     slot_v, length_v, msg_flat, msg, meta_v, meta, inverse_v, inverse,
     x, cent, slotrecv, slot_s, c0send, c0recv, start, osend, orecv, cur,
     ysend, yrecv, wbuf, rsend, rrecv, rscale,
-    load_sem, slot_send, slot_recv, c0_send, c0_recv, o_send, o_recv,
+    load_sem, ring_sem, slot_send, slot_recv, c0_send, c0_recv, o_send, o_recv,
     r_send, r_recv, y_send, y_recv, w_send, w_recv,
 ):
     parents, block, width = x.shape
@@ -45,8 +45,50 @@
     me = lax.axis_index("dp")
     g = lax.axis_index("grp")
 
-    def peer(i):
-        return lax.rem(me + lax.rem(i * stride, n), n)
+    lines, planes, cores = shape
+    side = lines * cores
+    my_core = lax.rem(me, cores)
+    my_plane = lax.rem(lax.div(me, cores), planes)
+    my_line = lax.div(me, cores * planes)
+
+    def peer(away, k):
+        line = lax.rem(my_line + lax.div(k, cores), lines)
+        plane = lax.rem(my_plane + away, planes)
+        core = lax.rem(my_core + lax.rem(k, cores), cores)
+        return (line * planes + plane) * cores + core
+
+    def each(distance, act):
+        def call(away, k, here, there):
+            line = lax.rem(lines - lax.div(k, cores), lines)
+            core = lax.rem(cores - lax.rem(k, cores), cores)
+            act(peer(away, k), here * side + k, there * side + line * cores + core)
+
+        if distance == 0:
+            pl.loop(1, side)(lambda k: call(0, k, 0, 0))
+        elif 2 * distance == planes:
+            pl.loop(0, side)(lambda k: call(distance, k, planes - 1, planes - 1))
+        else:
+
+            @pl.loop(0, 2 * side)
+            def _(i):
+                turn = lax.rem(i, 2)
+                low = 2 * distance - 1
+                call(distance + turn * (planes - 2 * distance), lax.div(i, 2), low + turn, low + 1 - turn)
+
+    reach = planes // 2
+    near_rows = 3 * side
+
+    def near(act):
+        each(1, act)
+        each(0, act)
+
+    def far(act):
+        for distance in range(reach, 1, -1):
+            each(distance, act)
+
+    def everyone(act):
+        far(act)
+        near(act)
 
     def mate(i):
         return lax.rem(g + i, groups)
@@ -61,9 +103,9 @@
 
     barrier = pltpu.get_barrier_semaphore()
 
-    @pl.loop(1, n)
-    def _(i):
-        pl.semaphore_signal(barrier, inc=1, device_id=(peer(i), g), device_id_type=MESH)
+    @near
+    def _(p, here, there):
+        pl.semaphore_signal(barrier, inc=1, device_id=(p, g), device_id_type=MESH)
 
     @pl.loop(1, groups)
     def _(i):
@@ -106,7 +148,52 @@
     def _(h):
         msg[h] = msg_flat[pl.ds(h, 1), :]
 
-    slotrecv[me] = msg[me]
+    slotrecv[0] = msg[me]
+    pl.semaphore_wait(barrier, near_rows - 1 + groups - 1)
+
+    def ask(k):
+        def send(p, here, there):
+            pltpu.make_async_remote_copy(
+                src_ref=msg.at[p], dst_ref=slotrecv.at[there],
+                send_sem=slot_send, recv_sem=slot_recv.at[k],
+                device_id=(p, g), device_id_type=MESH,
+            ).start()
+
+        return send
+
+    near(ask(0))
+    for distance in range(2, reach + 1):
+        ring = ring_sem.at[distance - 2]
+        for away in (1, planes - 1):
+            pl.semaphore_signal(ring, inc=1, device_id=(peer(away, 0), g), device_id_type=MESH)
+        pl.semaphore_wait(ring, 2)
+        each(distance, ask(1))
+
+    def serve(j, who):
+        @who
+        def _(p, here, there):
+            c0send[j, p] = cent[jnp.minimum(slot_s[here, 0, j], parents - 1)]
+
+        @who
+        def _(p, here, there):
+            pltpu.make_async_remote_copy(
+                src_ref=c0send.at[j, p], dst_ref=c0recv.at[j, me],
+                send_sem=c0_send.at[j], recv_sem=c0_recv.at[j],
+                device_id=(p, g), device_id_type=MESH,
+            ).start()
+
+    def to_scalars(first_row, rows, k):
+        part = pl.ds(first_row, rows)
+        load(slotrecv.at[part], slot_s.at[part], k).wait()
+
+    load_c.wait()
+    wait_bytes(slotrecv.at[pl.ds(0, near_rows - 1)], slot_recv.at[0])
+    to_scalars(0, near_rows, 5)
+
+    @pl.loop(0, CAP)
+    def _(j):
+        c0recv[j, me] = cent[jnp.minimum(slot_s[0, 0, j], parents - 1)]
+        serve(j, near)
 
     within = count((order == order_row) & (lan < sub), 1)
     hit = order * chunk + within == lan
@@ -117,50 +204,27 @@
         meta_v[3 + j] = jnp.sum(jnp.where(hit, within, 0), axis=0, keepdims=True)
     to_meta = load(meta_v, meta, 4)
 
-    pl.semaphore_wait(barrier, n - 1 + groups - 1)
-
-    @pl.loop(1, n)
-    def _(i):
-        p = peer(i)
-        pltpu.make_async_remote_copy(
-            src_ref=msg.at[p], dst_ref=slotrecv.at[me],
-            send_sem=slot_send, recv_sem=slot_recv,
-            device_id=(p, g), device_id_type=MESH,
-        ).start()
-
-    load_c.wait()
-    to_meta.wait()
-    wait_bytes(slotrecv.at[pl.ds(0, n - 1)], slot_recv)
-    to_scalars = load(slotrecv, slot_s, 5)
-    to_scalars.wait()
+
+    wait_bytes(slotrecv.at[pl.ds(near_rows, n - near_rows)], slot_recv.at[1])
+    to_scalars(near_rows, n - near_rows, 7)
 
     @pl.loop(0, CAP)
     def _(j):
-        @pl.loop(0, n, step=4)
-        def _(h):
-            for k in range(4):
-                slot = jnp.minimum(slot_s[h + k, 0, j], parents - 1)
-                c0send[j, h + k] = cent[slot]
-
-        c0recv[j, me] = c0send[j, me]
-
-        @pl.loop(1, n)
-        def _(i):
-            p = peer(i)
-            pltpu.make_async_remote_copy(
-                src_ref=c0send.at[j, p], dst_ref=c0recv.at[j, me],
-                send_sem=c0_send.at[j], recv_sem=c0_recv.at[j],
-                device_id=(p, g), device_id_type=MESH,
-            ).start()
+        serve(j, far)
+
+    to_meta.wait()
 
     row = iota((1, parents), 1)
 
-    def note(s, found):
+    def note(p, here, there):
+        found = inverse_v[0]
         for j in range(CAP):
-            found = jnp.where(row == slot_s[s, 0, j], j * n + s, found)
-        return found
-
-    inverse_v[0] = lax.fori_loop(0, n, note, jnp.zeros((1, parents), jnp.int32))
+            found = jnp.where(row == slot_s[here, 0, j], j * n + p, found)
+        inverse_v[0] = found
+
+    inverse_v[0] = jnp.zeros((1, parents), jnp.int32)
+    note(me, 0, 0)
+    everyone(note)
     to_inverse = load(inverse_v, inverse, 6)
 
     lane = iota((children, LANES), 1)
@@ -322,9 +386,8 @@
 
         orecv[j * n + me] = osend[j, me]
 
-        @pl.loop(1, n)
-        def _(i):
-            p = peer(i)
+        @everyone
+        def _(p, here, there):
             pltpu.make_async_remote_copy(
                 src_ref=osend.at[j, p], dst_ref=orecv.at[j * n + me],
                 send_sem=o_send.at[j], recv_sem=o_recv.at[j],
@@ -370,7 +433,7 @@
     groups = lax.axis_size("grp")
     chunk = parents // CAP
     per_owner = chunk // 2 // groups
-    stride = 27 if n % 27 else 1
+    shape = (4, 8, 2) if n == 64 else (1, n // 2, 2)
 
     dma = pltpu.SemaphoreType.DMA
     vmem, smem = pltpu.VMEM, pltpu.SMEM
@@ -379,7 +442,7 @@
     bf16, f32, i32 = jnp.bfloat16, jnp.float32, jnp.int32
     by_owner = (CAP, ITERS, groups, per_owner + 1, children, LANES)
     return pl.pallas_call(
-        functools.partial(kernel, n, groups, stride),
+        functools.partial(kernel, n, groups, shape),
         out_shape=jax.ShapeDtypeStruct(centroids.shape, bf16),
         in_specs=[pl.BlockSpec(memory_space=pl.ANY)] * 4,
         out_specs=pl.BlockSpec(memory_space=vmem),
@@ -408,15 +471,28 @@
             vmem((groups, CAP * per_owner, LANES), f32),
             vmem((groups, CAP * per_owner, LANES), f32),
             vmem((CAP * per_owner, LANES), f32),
-            dma((7,)),
-            dma, dma,
+            dma((8,)),
+            pltpu.SemaphoreType.REGULAR((shape[1] // 2 - 1,)),
+            dma, dma((2,)),
             dma((CAP,)), dma((CAP,)), dma((CAP,)), dma((CAP,)),
             dma, dma,
             dma((CAP, ITERS)), dma((CAP, ITERS)), dma((CAP, ITERS)), dma((CAP, ITERS)),
         ],
-        compiler_params=pltpu.CompilerParams(collective_id=0, has_side_effects=True),
+        compiler_params=pltpu.CompilerParams(
+            collective_id=0, has_side_effects=True, vmem_limit_bytes=28 << 20
+        ),
         name="refine",
-    )(parent_slot.reshape(1, parents), lengths.reshape(1, parents), embeddings, centroids)
+    )(
+        *(
+            pltpu.with_memory_space_constraint(value, pltpu.HBM)
+            for value in (
+                parent_slot.reshape(1, parents),
+                lengths.reshape(1, parents),
+                embeddings,
+                centroids,
+            )
+        )
+    )
 
 
 def solution(mesh):

time: 115 us -> 111 us (0.965)
  Pallas kernels: 113 us -> 110 us
  local copies, waits for them, and re-layouts: 2.26 us -> 0.97 us
    pallas_call x1, Pallas kernels: 113 us -> 110 us  [on_device(): pl.pallas_call(functools.partial(kernel, n, groups, shape), out_shape=jax...]
    unnamed x1, local copies, waits for them, and re-layouts: 2.26 us -> 0.97 us
where the time goes in v3:
time: 111 us
  Pallas kernels  110 us (99%)
    pallas_call x1, Pallas kernels, on_device(): pl.pallas_call(functools.partial(kernel, n, groups, shape), out_shape=jax...  110 us

profile of v3, /device:TPU:1, one launch (start us, length us, event | category | flops | bytes accessed | tf_op | source)
XLA Modules:
  0.0 111.0 jit_solution(14183719281432976218)
XLA Ops:
  0.0 110.0 %refine.1 = bf16[128,16,256]{2,1,0:T(8,128)(2,1)S(1)} custom-call(s32[1,128]{1,0:T(1,128)} %bitcast.2, s32[1,128]{1,0:T(1,128)} %bitcast.3, bf16[128,64,256]{2,1,0:T(8,128)(2,1)} %x_hbm.1, bf16[128,16,256]{2,1,0:T(8,128)(2,1)} %cent_hbm.1), custom_call_target="tpu_custom_call" | custom-call | tf_op jit(solution)/shard_map/refine/pallas_call | solution.py:444
  110.0 1.0 copy.6

commit v4 on v3

--- a/solution.py
+++ b/solution.py
@@ -90,6 +90,24 @@
         far(act)
         near(act)
 
+    def mixed(act):
+        @pl.loop(1, n)
+        def _(i):
+            m = lax.rem(i, planes)
+            odd = lax.rem(m, 2)
+            half = lax.div(m + 1, 2)
+            act(peer(lax.rem(odd * half + (1 - odd) * (planes - half), planes), lax.div(i, planes)), 0, 0)
+
+    def far_mixed(act):
+        @pl.loop(0, side * (planes - 3))
+        def _(i):
+            act(peer(2 + lax.rem(i, planes - 3), lax.div(i, planes - 3)), row_of(2 + lax.rem(i, planes - 3), lax.div(i, planes - 3)), 0)
+
+    def row_of(away, k):
+        low = 2 * away - 1
+        high = 2 * (planes - away)
+        return lax.min(low, high) * side + k
+
     def mate(i):
         return lax.rem(g + i, groups)
 
@@ -161,13 +179,20 @@
 
         return send
 
+    def tell(distance):
+        for away in (1, planes - 1):
+            pl.semaphore_signal(
+                ring_sem.at[distance - 2], inc=1,
+                device_id=(peer(away, 0), g), device_id_type=MESH,
+            )
+
+    tell(2)
     near(ask(0))
     for distance in range(2, reach + 1):
-        ring = ring_sem.at[distance - 2]
-        for away in (1, planes - 1):
-            pl.semaphore_signal(ring, inc=1, device_id=(peer(away, 0), g), device_id_type=MESH)
-        pl.semaphore_wait(ring, 2)
-        each(distance, ask(1))
+        pl.semaphore_wait(ring_sem.at[distance - 2], 2)
+        if distance < reach:
+            tell(distance + 1)
+        each(distance, ask(distance - 1))
 
     def serve(j, who):
         @who
@@ -194,6 +219,17 @@
     def _(j):
         c0recv[j, me] = cent[jnp.minimum(slot_s[0, 0, j], parents - 1)]
         serve(j, near)
+
+    for distance in range(2, reach + 1):
+        first_row = (2 * distance - 1) * side
+        rows = side if 2 * distance == planes else 2 * side
+        wait_bytes(slotrecv.at[pl.ds(first_row, rows)], slot_recv.at[distance - 1])
+        to_scalars(first_row, rows, 5 + distance)
+        serve(0, functools.partial(each, distance))
+
+    @pl.loop(1, CAP)
+    def _(j):
+        serve(j, far_mixed)
 
     within = count((order == order_row) & (lan < sub), 1)
     hit = order * chunk + within == lan
@@ -204,16 +240,6 @@
         meta_v[3 + j] = jnp.sum(jnp.where(hit, within, 0), axis=0, keepdims=True)
     to_meta = load(meta_v, meta, 4)
 
-
-    wait_bytes(slotrecv.at[pl.ds(near_rows, n - near_rows)], slot_recv.at[1])
-    to_scalars(near_rows, n - near_rows, 7)
-
-    @pl.loop(0, CAP)
-    def _(j):
-        serve(j, far)
-
-    to_meta.wait()
-
     row = iota((1, parents), 1)
 
     def note(p, here, there):
@@ -226,6 +252,7 @@
     note(me, 0, 0)
     everyone(note)
     to_inverse = load(inverse_v, inverse, 6)
+    to_meta.wait()
 
     lane = iota((children, LANES), 1)
     first = lane < block
@@ -386,7 +413,7 @@
 
         orecv[j * n + me] = osend[j, me]
 
-        @everyone
+        @mixed
         def _(p, here, there):
             pltpu.make_async_remote_copy(
                 src_ref=osend.at[j, p], dst_ref=orecv.at[j * n + me],
@@ -471,9 +498,9 @@
             vmem((groups, CAP * per_owner, LANES), f32),
             vmem((groups, CAP * per_owner, LANES), f32),
             vmem((CAP * per_owner, LANES), f32),
-            dma((8,)),
+            dma((6 + shape[1] // 2,)),
             pltpu.SemaphoreType.REGULAR((shape[1] // 2 - 1,)),
-            dma, dma((2,)),
+            dma, dma((shape[1] // 2,)),
             dma((CAP,)), dma((CAP,)), dma((CAP,)), dma((CAP,)),
             dma, dma,
             dma((CAP, ITERS)), dma((CAP, ITERS)), dma((CAP, ITERS)), dma((CAP, ITERS)),

time: 111 us -> 109 us (0.982)
  Pallas kernels: 110 us -> 108 us
    pallas_call x1, Pallas kernels: 110 us -> 108 us  [on_device(): pl.pallas_call(functools.partial(kernel, n, groups, shape), out_shape=jax...]
where the time goes in v4:
time: 109 us
  Pallas kernels  108 us (99%)
    pallas_call x1, Pallas kernels, on_device(): pl.pallas_call(functools.partial(kernel, n, groups, shape), out_shape=jax...  108 us

profile of v4, /device:TPU:1, one launch (start us, length us, event | category | flops | bytes accessed | tf_op | source)
XLA Modules:
  0.0 109.4 jit_solution(6521725320278694264)
XLA Ops:
  0.0 108.4 %refine.1 = bf16[128,16,256]{2,1,0:T(8,128)(2,1)S(1)} custom-call(s32[1,128]{1,0:T(1,128)} %bitcast.2, s32[1,128]{1,0:T(1,128)} %bitcast.3, bf16[128,64,256]{2,1,0:T(8,128)(2,1)} %x_hbm.1, bf16[128,16,256]{2,1,0:T(8,128)(2,1)} %cent_hbm.1), custom_call_target="tpu_custom_call" | custom-call | tf_op jit(solution)/shard_map/refine/pallas_call | solution.py:471
  108.4 1.0 copy.6
